TPU v7x, 32 devices: a whole 2x2x4 slice. The times are simulated.
32 devices in a mesh: dp: 8 (over y, x, core), tensor: 4 (over z).
Axes of the slice: x: 2, y: 2, z: 4, core: 2. Of those that a mesh axis runs over, the one named last changes fastest.
Arguments:
- block_in: float32 [4096, 1024], P(('dp', 'tensor')), may hold values from -6 to 6
- cotangent: float32 [4096, 1024], P(('dp', 'tensor')), may hold values from -6 to 6
- routes: int32 [4096, 8], P('dp'), may hold values from 0 to 15, all different within a row; in each aligned block of 512 rows (0 to 511, 512 to 1023, ...) at most 288 rows name the same one
- gate_weights: float32 [4096, 8], P('dp'), may hold values from 0.02 to 0.3
- norm_gains: float32 [2, 1024], P(None, 'dp'), may hold values from 0.5 to 1.5
- attention_weight: float32 [4, 1024, 512], P(None, 'dp', 'tensor'), may hold values from -0.1875 to 0.1875
- output_weight: float32 [2, 1024, 512], P(None, 'dp', 'tensor'), may hold values from -0.75 to 0.75
- w_gate_up: float32 [16, 2, 1024, 512], P(None, None, 'dp', 'tensor'), may hold values from -0.1875 to 0.1875
- w_down: float32 [16, 1024, 512], P(None, 'dp', 'tensor'), may hold values from -0.75 to 0.75
- m_gains: float32 [2, 1024], P(None, 'dp'), may hold values from -128 to 128
- v_gains: float32 [2, 1024], P(None, 'dp'), may hold values from 100 to 10000
- attention_first_moment: float32 [4, 1024, 512], P(None, 'dp', 'tensor'), may hold values from -12 to 12
- attention_second_moment: float32 [4, 1024, 512], P(None, 'dp', 'tensor'), may hold values from 1 to 100
- output_first_moment: float32 [2, 1024, 512], P(None, 'dp', 'tensor'), may hold values from -16 to 16
- output_second_moment: float32 [2, 1024, 512], P(None, 'dp', 'tensor'), may hold values from 1 to 100
- m_gate_up: float32 [16, 2, 1024, 512], P(None, None, 'dp', 'tensor'), may hold values from -32 to 32
- v_gate_up: float32 [16, 2, 1024, 512], P(None, None, 'dp', 'tensor'), may hold values from 10 to 1000
- m_down: float32 [16, 1024, 512], P(None, 'dp', 'tensor'), may hold values from -12 to 12
- v_down: float32 [16, 1024, 512], P(None, 'dp', 'tensor'), may hold values from 1 to 100
Outputs:
- block_out: float32 [4096, 1024], P(('dp', 'tensor'))
- input_grad: float32 [4096, 1024], P(('dp', 'tensor'))
- grad_gains: float32 [2, 1024], P(None, 'dp')
- grad_attn: float32 [4, 1024, 512], P(None, 'dp', 'tensor')
- grad_out: float32 [2, 1024, 512], P(None, 'dp', 'tensor')
- grad_gate_up: float32 [16, 2, 1024, 512], P(None, None, 'dp', 'tensor')
- grad_down: float32 [16, 1024, 512], P(None, 'dp', 'tensor')
- new_gains: float32 [2, 1024], P(None, 'dp')
- new_attn: float32 [4, 1024, 512], P(None, 'dp', 'tensor')
- new_out: float32 [2, 1024, 512], P(None, 'dp', 'tensor')
- new_gate_up: float32 [16, 2, 1024, 512], P(None, None, 'dp', 'tensor')
- new_down: float32 [16, 1024, 512], P(None, 'dp', 'tensor')
- new_m_gains: float32 [2, 1024], P(None, 'dp')
- new_v_gains: float32 [2, 1024], P(None, 'dp')
- new_m_attn: float32 [4, 1024, 512], P(None, 'dp', 'tensor')
- new_v_attn: float32 [4, 1024, 512], P(None, 'dp', 'tensor')
- new_m_out: float32 [2, 1024, 512], P(None, 'dp', 'tensor')
- new_v_out: float32 [2, 1024, 512], P(None, 'dp', 'tensor')
- new_m_gate_up: float32 [16, 2, 1024, 512], P(None, None, 'dp', 'tensor')
- new_v_gate_up: float32 [16, 2, 1024, 512], P(None, None, 'dp', 'tensor')
- new_m_down: float32 [16, 1024, 512], P(None, 'dp', 'tensor')
- new_v_down: float32 [16, 1024, 512], P(None, 'dp', 'tensor')
Inputs may be any that keep to these rules, and one draw needn't show every extreme that they name: `routes`: each row names 8 different experts. Within each aligned block of 512 rows no expert is named by more than 288 rows, and in some block one expert is named by exactly 288 rows.
All inputs are finite; a program needn't handle non-finite values.
Results may differ from a plain program's by a relative error of at most 0.015.
The roundings to bfloat16 on the way count: a program that leaves them out, or rounds other values in their place, can miss the bound.
Values may be sent and summed in bfloat16 or wider, within the bound.
A program may use at most 192 MiB of HBM per device.

v0:
```python
import jax
import jax.numpy as jnp
from jax import lax
from jax.sharding import PartitionSpec as P

HEAD_SIZE = 64
E = 16
SEQ = 512
STEP = 3
CAP = 288
norm_eps = 1e-05
beta_one = 0.9
beta_two = 0.95
adam_eps = 1e-08
rate_matrix = 0.02
rate_gain = 0.2
decay_matrix = 0.1
rope_base = 10000.0


def rope_tables(length, width):
    half_width = width // 2
    frequency = rope_base ** (-(2.0 * jnp.arange(half_width, dtype=jnp.float32)) / width)
    angles = jnp.arange(length, dtype=jnp.float32)[:, None] * frequency[None, :]
    return (jnp.cos(angles)[:, None, :], jnp.sin(angles)[:, None, :])


def rotate(vectors, cos_table, sine_table):
    half_width = vectors.shape[-1] // 2
    lower_half = vectors[..., :half_width]
    upper_half = vectors[..., half_width:]
    return jnp.concatenate(
        [
            lower_half * cos_table - upper_half * sine_table,
            upper_half * cos_table + lower_half * sine_table,
        ],
        axis=-1,
    )


def unrotate(vectors, cos_table, sine_table):
    half_width = vectors.shape[-1] // 2
    lower_half = vectors[..., :half_width]
    upper_half = vectors[..., half_width:]
    return jnp.concatenate(
        [
            lower_half * cos_table + upper_half * sine_table,
            upper_half * cos_table - lower_half * sine_table,
        ],
        axis=-1,
    )


def causal_scores(queries, keys_rot):
    scale = queries.shape[-1] ** (-0.5)
    scores = (
        jnp.einsum("jqgh,kgh->jgqk", queries, keys_rot, preferred_element_type=jnp.float32) * scale
    )
    length = scores.shape[-1]
    allowed = lax.broadcasted_iota(jnp.int32, (length, length), 0) >= lax.broadcasted_iota(
        jnp.int32, (length, length), 1
    )
    return jnp.where(allowed, scores, -jnp.inf)


def attend(items):
    queries, keys_rot, values = items
    scores = causal_scores(queries, keys_rot)
    log_totals = jax.nn.logsumexp(scores, axis=-1)
    softmax_b = jnp.exp(scores - log_totals[..., None]).astype(jnp.bfloat16)
    attended = jnp.einsum(
        "jgqk,kgh->jqgh", softmax_b, values, preferred_element_type=jnp.float32
    ).astype(jnp.bfloat16)
    return (attended, log_totals)


def attend_back(items):
    queries, keys_rot, values, attended, log_totals, attended_cot = items
    scale = queries.shape[-1] ** (-0.5)
    scores = causal_scores(queries, keys_rot)
    softmax_f = jnp.exp(scores - log_totals[..., None])
    softmax_b = softmax_f.astype(jnp.bfloat16)
    value_cot = jnp.einsum(
        "jgqk,jqgh->kgh", softmax_b, attended_cot, preferred_element_type=jnp.float32
    )
    weight_cot = jnp.einsum(
        "jqgh,kgh->jgqk", attended_cot, values, preferred_element_type=jnp.float32
    )
    row_dots = jnp.einsum(
        "jqgh,jqgh->jgq", attended_cot, attended, preferred_element_type=jnp.float32
    )
    score_cot = (softmax_f * (weight_cot - row_dots[..., None])).astype(jnp.bfloat16)
    query_cot = (
        jnp.einsum("jgqk,kgh->jqgh", score_cot, keys_rot, preferred_element_type=jnp.float32)
        * scale
    )
    key_cot = (
        jnp.einsum("jgqk,jqgh->kgh", score_cot, queries, preferred_element_type=jnp.float32) * scale
    )
    return (query_cot, key_cot, value_cot)


def slot_table(route_rows, gate_rows, tok_count):
    hits = (route_rows[:, :, None] == jnp.arange(E, dtype=jnp.int32)[None, None, :]).astype(
        jnp.int32
    )
    per_token = jnp.sum(hits, axis=1, dtype=jnp.int32)
    before = jnp.cumsum(per_token, axis=0, dtype=jnp.int32) - per_token
    position = jnp.sum(hits * before[:, None, :], axis=2, dtype=jnp.int32)
    flat_slot = (route_rows * CAP + position).reshape(-1)
    owner = jnp.broadcast_to(
        jnp.arange(tok_count, dtype=jnp.int32)[:, None], route_rows.shape
    ).reshape(-1)
    slot_token = jnp.full((E * CAP,), tok_count, jnp.int32).at[flat_slot].set(owner)
    slot_weight = jnp.zeros((E * CAP,), jnp.float32).at[flat_slot].set(gate_rows.reshape(-1))
    return (slot_token, slot_weight)


def fetch_experts(w_gate_up, w_down, start_expert, per_turn):
    gate_up_part = w_gate_up[start_expert : start_expert + per_turn].astype(jnp.bfloat16)
    down_part = w_down[start_expert : start_expert + per_turn].astype(jnp.bfloat16)
    return (
        lax.all_gather(gate_up_part, "dp", axis=2, tiled=True),
        lax.all_gather(down_part, "dp", axis=1, tiled=True),
    )


def adamw_update(weight, moment_one, moment_two, gradient, rate, decay):
    new_one = beta_one * moment_one + (1.0 - beta_one) * gradient
    new_two = beta_two * moment_two + (1.0 - beta_two) * gradient * gradient
    corrected_one = new_one / (1.0 - beta_one**STEP)
    corrected_two = new_two / (1.0 - beta_two**STEP)
    new_weight = weight - rate * (
        corrected_one / (jnp.sqrt(corrected_two) + adam_eps) + decay * weight
    )
    return (new_weight, new_one, new_two)


def local(
    block_in,
    cotangent,
    routes,
    gate_weights,
    norm_gains,
    attention_weight,
    output_weight,
    w_gate_up,
    w_down,
    m_gains,
    v_gains,
    attention_first_moment,
    attention_second_moment,
    output_first_moment,
    output_second_moment,
    m_gate_up,
    v_gate_up,
    m_down,
    v_down,
):
    gains_all, attn_all, out_all = (
        lax.all_gather(norm_gains.astype(jnp.bfloat16), "dp", axis=1, tiled=True),
        lax.all_gather(attention_weight.astype(jnp.bfloat16), "dp", axis=1, tiled=True),
        lax.all_gather(output_weight.astype(jnp.bfloat16), "dp", axis=1, tiled=True),
    )
    tok_count = routes.shape[0]
    seq_count = tok_count // SEQ
    width = block_in.shape[1]
    kv_count = attn_all.shape[2] // HEAD_SIZE
    cos_table, sine_table = rope_tables(SEQ, HEAD_SIZE)
    gain_one = gains_all[0].astype(jnp.float32)
    gain_two = gains_all[1].astype(jnp.float32)
    inv_one = lax.rsqrt(jnp.mean(block_in * block_in, axis=1, keepdims=True) + norm_eps)
    normed_one = (block_in * inv_one * gain_one).astype(jnp.bfloat16)
    tokens_one = lax.all_gather(normed_one, "tensor", axis=0, tiled=True)
    projected = jnp.einsum("td,zdc->ztc", tokens_one, attn_all, preferred_element_type=jnp.float32)
    head_vals = projected.reshape(4, seq_count, SEQ, kv_count, HEAD_SIZE)
    queries = (
        rotate(head_vals[0:2], cos_table, sine_table).astype(jnp.bfloat16).transpose(1, 0, 2, 3, 4)
    )
    keys_rot = rotate(head_vals[2], cos_table, sine_table).astype(jnp.bfloat16)
    values = head_vals[3].astype(jnp.bfloat16)
    attended, log_totals = lax.map(attend, (queries, keys_rot, values))
    attended_flat = attended.transpose(1, 0, 2, 3, 4).reshape(2, tok_count, kv_count * HEAD_SIZE)
    partial_value = jnp.einsum(
        "jtc,jdc->td", attended_flat, out_all, preferred_element_type=jnp.float32
    )
    residual = block_in + lax.psum_scatter(partial_value, "tensor", scatter_dimension=0, tiled=True)
    inv_two = lax.rsqrt(jnp.mean(residual * residual, axis=1, keepdims=True) + norm_eps)
    normed_two = (residual * inv_two * gain_two).astype(jnp.bfloat16)
    tokens_two = lax.all_gather(normed_two, "tensor", axis=0, tiled=True)
    slot_token, slot_weight = slot_table(routes, gate_weights, tok_count)
    padded = jnp.concatenate([tokens_two, jnp.zeros((1, width), jnp.bfloat16)], axis=0)
    expert_in = padded[slot_token].reshape(E, CAP, width)
    per_turn = 8
    mixture = jnp.zeros((tok_count + 1, width), jnp.float32)
    saved_acts = []
    for start_expert in range(0, E, per_turn):
        gate_up_g, down_g = fetch_experts(w_gate_up, w_down, start_expert, per_turn)
        inputs = expert_in[start_expert : start_expert + per_turn]
        gate_up = jnp.einsum(
            "ecd,ezdf->zecf", inputs, gate_up_g, preferred_element_type=jnp.float32
        )
        hidden = (jax.nn.silu(gate_up[0]) * gate_up[1]).astype(jnp.bfloat16)
        expert_out = jnp.einsum("ecf,edf->ecd", hidden, down_g, preferred_element_type=jnp.float32)
        slot_rows = slot_token[start_expert * CAP : (start_expert + per_turn) * CAP]
        row_weight = slot_weight[start_expert * CAP : (start_expert + per_turn) * CAP]
        mixture = mixture.at[slot_rows].add(expert_out.reshape(-1, width) * row_weight[:, None])
        saved_acts.append((gate_up, hidden))
    block_out = residual + lax.psum_scatter(
        mixture[:tok_count].astype(jnp.bfloat16), "tensor", scatter_dimension=0, tiled=True
    ).astype(jnp.float32)
    cot_all = lax.all_gather(cotangent, "tensor", axis=0, tiled=True)
    cot_pad = jnp.concatenate([cot_all, jnp.zeros((1, width), jnp.float32)], axis=0)
    slot_cot = (
        (slot_weight[:, None] * cot_pad[slot_token]).astype(jnp.bfloat16).reshape(E, CAP, width)
    )
    back_sum = jnp.zeros((tok_count + 1, width), jnp.float32)
    parts_gate_up = []
    parts_down = []
    for turn_index, start_expert in enumerate(range(0, E, per_turn)):
        gate_up_g, down_g = fetch_experts(w_gate_up, w_down, start_expert, per_turn)
        gate_up, hidden = saved_acts[turn_index]
        gate_vals = gate_up[0]
        up_vals = gate_up[1]
        inputs = expert_in[start_expert : start_expert + per_turn]
        turn_cot = slot_cot[start_expert : start_expert + per_turn]
        down_local = jnp.einsum(
            "ecd,ecf->edf", turn_cot, hidden, preferred_element_type=jnp.float32
        )
        hidden_cot = jnp.einsum(
            "ecd,edf->ecf", turn_cot, down_g, preferred_element_type=jnp.float32
        )
        sigmoid_vals = jax.nn.sigmoid(gate_vals)
        gate_cot = (
            hidden_cot * up_vals * sigmoid_vals * (1.0 + gate_vals * (1.0 - sigmoid_vals))
        ).astype(jnp.bfloat16)
        up_cot = (hidden_cot * gate_vals * sigmoid_vals).astype(jnp.bfloat16)
        both_cot = jnp.stack([gate_cot, up_cot])
        gate_up_local = jnp.einsum(
            "ecd,zecf->ezdf", inputs, both_cot, preferred_element_type=jnp.float32
        )
        input_cot = jnp.einsum(
            "zecf,ezdf->ecd", both_cot, gate_up_g, preferred_element_type=jnp.float32
        )
        slot_rows = slot_token[start_expert * CAP : (start_expert + per_turn) * CAP]
        back_sum = back_sum.at[slot_rows].add(input_cot.reshape(-1, width))
        summed_gate_up, summed_down = (
            lax.psum_scatter(gate_up_local, "dp", scatter_dimension=2, tiled=True),
            lax.psum_scatter(down_local, "dp", scatter_dimension=1, tiled=True),
        )
        parts_gate_up.append(summed_gate_up)
        parts_down.append(summed_down)
    grad_gate_up = jnp.concatenate(parts_gate_up, axis=0)
    grad_down = jnp.concatenate(parts_down, axis=0)
    normed_two_cot = lax.psum_scatter(
        back_sum[:tok_count], "tensor", scatter_dimension=0, tiled=True
    )
    scaled_two = gain_two * normed_two_cot
    residual_cot = (
        cotangent
        + inv_two * scaled_two
        - residual * inv_two**3 * jnp.mean(scaled_two * residual, axis=1, keepdims=True)
    )
    resid_all = lax.all_gather(residual_cot.astype(jnp.bfloat16), "tensor", axis=0, tiled=True)
    out_local = jnp.einsum(
        "td,jtc->jdc", resid_all, attended_flat, preferred_element_type=jnp.float32
    )
    attended_cot = jnp.einsum(
        "td,jdc->jtc", resid_all, out_all, preferred_element_type=jnp.float32
    ).astype(jnp.bfloat16)
    attended_cot = attended_cot.reshape(2, seq_count, SEQ, kv_count, HEAD_SIZE).transpose(
        1, 0, 2, 3, 4
    )
    query_cot, key_cot, value_cot = lax.map(
        attend_back, (queries, keys_rot, values, attended, log_totals, attended_cot)
    )
    query_plain = (
        unrotate(query_cot, cos_table, sine_table)
        .transpose(1, 0, 2, 3, 4)
        .reshape(2, tok_count, kv_count * HEAD_SIZE)
    )
    key_plain = unrotate(key_cot, cos_table, sine_table).reshape(1, tok_count, kv_count * HEAD_SIZE)
    proj_cot = jnp.concatenate(
        [query_plain, key_plain, value_cot.reshape(1, tok_count, kv_count * HEAD_SIZE)], axis=0
    ).astype(jnp.bfloat16)
    attn_local = jnp.einsum("td,ztc->zdc", tokens_one, proj_cot, preferred_element_type=jnp.float32)
    norm_terms = jnp.einsum("ztc,zdc->td", proj_cot, attn_all, preferred_element_type=jnp.float32)
    normed_one_cot = lax.psum_scatter(
        norm_terms.astype(jnp.bfloat16), "tensor", scatter_dimension=0, tiled=True
    ).astype(jnp.float32)
    scaled_one = gain_one * normed_one_cot
    input_grad = (
        residual_cot
        + inv_one * scaled_one
        - block_in * inv_one**3 * jnp.mean(scaled_one * block_in, axis=1, keepdims=True)
    )
    gain_local = jnp.stack(
        [
            jnp.sum(normed_one_cot * block_in * inv_one, axis=0),
            jnp.sum(normed_two_cot * residual * inv_two, axis=0),
        ]
    )
    gain_part, grad_attn, grad_out = (
        lax.psum_scatter(gain_local, "dp", scatter_dimension=1, tiled=True),
        lax.psum_scatter(attn_local, "dp", scatter_dimension=1, tiled=True),
        lax.psum_scatter(out_local, "dp", scatter_dimension=1, tiled=True),
    )
    grad_gains = lax.psum(gain_part, "tensor")
    new_gains, new_m_gains, new_v_gains = adamw_update(
        norm_gains, m_gains, v_gains, grad_gains, rate_gain, 0.0
    )
    new_attn, new_m_attn, new_v_attn = adamw_update(
        attention_weight,
        attention_first_moment,
        attention_second_moment,
        grad_attn,
        rate_matrix,
        decay_matrix,
    )
    new_out, new_m_out, new_v_out = adamw_update(
        output_weight,
        output_first_moment,
        output_second_moment,
        grad_out,
        rate_matrix,
        decay_matrix,
    )
    new_gate_up, new_m_gate_up, new_v_gate_up = adamw_update(
        w_gate_up, m_gate_up, v_gate_up, grad_gate_up, rate_matrix, decay_matrix
    )
    new_down, new_m_down, new_v_down = adamw_update(
        w_down, m_down, v_down, grad_down, rate_matrix, decay_matrix
    )
    return (
        block_out,
        input_grad,
        grad_gains,
        grad_attn,
        grad_out,
        grad_gate_up,
        grad_down,
        new_gains,
        new_attn,
        new_out,
        new_gate_up,
        new_down,
        new_m_gains,
        new_v_gains,
        new_m_attn,
        new_v_attn,
        new_m_out,
        new_v_out,
        new_m_gate_up,
        new_v_gate_up,
        new_m_down,
        new_v_down,
    )


def solution(mesh):
    return jax.shard_map(
        local,
        mesh=mesh,
        in_specs=(
            P(("dp", "tensor"), None),
            P(("dp", "tensor"), None),
            P("dp", None),
            P("dp", None),
            P(None, "dp"),
            P(None, "dp", "tensor"),
            P(None, "dp", "tensor"),
            P(None, None, "dp", "tensor"),
            P(None, "dp", "tensor"),
            P(None, "dp"),
            P(None, "dp"),
            P(None, "dp", "tensor"),
            P(None, "dp", "tensor"),
            P(None, "dp", "tensor"),
            P(None, "dp", "tensor"),
            P(None, None, "dp", "tensor"),
            P(None, None, "dp", "tensor"),
            P(None, "dp", "tensor"),
            P(None, "dp", "tensor"),
        ),
        out_specs=(
            P(("dp", "tensor"), None),
            P(("dp", "tensor"), None),
            P(None, "dp"),
            P(None, "dp", "tensor"),
            P(None, "dp", "tensor"),
            P(None, None, "dp", "tensor"),
            P(None, "dp", "tensor"),
            P(None, "dp"),
            P(None, "dp", "tensor"),
            P(None, "dp", "tensor"),
            P(None, None, "dp", "tensor"),
            P(None, "dp", "tensor"),
            P(None, "dp"),
            P(None, "dp"),
            P(None, "dp", "tensor"),
            P(None, "dp", "tensor"),
            P(None, "dp", "tensor"),
            P(None, "dp", "tensor"),
            P(None, None, "dp", "tensor"),
            P(None, None, "dp", "tensor"),
            P(None, "dp", "tensor"),
            P(None, "dp", "tensor"),
        ),
        check_vma=False,
    )
```

profile of v0, /device:TPU:0, one launch (start us, length us, event | category | flops | bytes accessed | tf_op | source)
XLA Modules:
  0.0 941.3 jit_solution(5812253227274895094)
XLA Ops:
  8.0 10.3 %all_gather.37 = bf16[2,1024]{1,0:T(2,128)(2,1)S(1)} all-gather(bf16[2,128]{1,0:T(2,128)(2,1)S(1)} %convert_element_type.103), channel_id=1, replica_groups=mesh['dp'=8,'tensor'=4] {'dp'}, dimensions={1}, use_global_device_ids=true | all-gather | bytes 4608 | tf_op jit(solution)/shard_map/all_gather | solution.py:161
  23.8 9.8 %all_gather.40 = bf16[2,1024,128]{2,1,0:T(8,128)(2,1)S(1)} all-gather(bf16[2,128,128]{2,1,0:T(8,128)(2,1)S(1)} %convert_element_type.110), channel_id=1, replica_groups=mesh['dp'=8,'tensor'=4] {'dp'}, dimensions={1}, use_global_device_ids=true | all-gather | bytes 589824 | tf_op jit(solution)/shard_map/all_gather | solution.py:163
  34.1 16.2 %all-gather.10.cloned.1.call-done = bf16[512,1024]{1,0:T(8,128)(2,1)} async-done(((bf16[128,1024]{1,0:T(8,128)(2,1)}), bf16[512,1024]{1,0:T(8,128)(2,1)}) %all-gather.10.cloned.1.call-update) | async-done | bytes 1048592 | tf_op jit(solution)/shard_map/all_gather | solution.py:174
  50.3 25.3 %all-gather.12.cloned.1.call-done = bf16[4,1024,128]{1,2,0:T(8,128)(2,1)} async-done(((bf16[4,128,128]{1,2,0:T(8,128)(2,1)}), bf16[4,1024,128]{1,2,0:T(8,128)(2,1)}) %all-gather.12.cloned.1.call-update) | async-done | bytes 1048592 | tf_op jit(solution)/shard_map/all_gather | solution.py:162
  86.5 43.2 %reduce-scatter.14.cloned.1.call-done = f32[128,1024]{1,0:T(8,128)} async-done(((f32[512,1024]{1,0:T(8,128)}), f32[128,1024]{1,0:T(8,128)}) %reduce-scatter.14.cloned.1.call-update) | async-done | bytes 524304 | tf_op jit(solution)/shard_map/reduce_scatter | solution.py:187
  139.9 15.5 %scatter_custom_fusion = s32[4608]{0:T(1024)S(1)} fusion(s32[4096]{0:T(1024)S(1)} %bitcast.271, s32[4096]{0:T(1024)S(1)} %reshape.349, s32[]{:T(128)} %constant.51.clone.1), kind=kCustom, calls=%fused_computation.145 | custom fusion | bytes 18436 | tf_op jit(solution)/shard_map/scatter | solution.py:114
  155.8 16.0 %scatter_custom_fusion.1 = f32[4608]{0:T(1024)S(1)} fusion(s32[4096]{0:T(1024)S(1)} %bitcast.272, f32[4096]{0:T(1024)S(1)} %reshape.357, f32[]{:T(128)} %constant.43.clone.1), kind=kCustom, calls=%fused_computation.143 | custom fusion | bytes 18436 | tf_op jit(solution)/shard_map/scatter | solution.py:115
  171.8 4.1 all-gather.24.cloned.1.call-done
  177.7 15.2 %gather_fusion.1 = f32[4608,1024]{1,0:T(8,128)} fusion(f32[513,1024]{1,0:T(8,128)S(1)} %concatenate.53, s32[5120]{0:T(1024)S(1)} %pad_clamp_fusion), kind=kCustom, calls=%fused_computation.1 | custom fusion | bytes 37767168 | tf_op jit(solution)/shard_map/gather | solution.py:215
  192.9 8.0 multiply_convert_fusion
  200.9 4.8 fusion.72
  207.0 14.9 %gather_fusion = bf16[4608,1024]{1,0:T(8,128)(2,1)} fusion(bf16[513,1024]{1,0:T(8,128)(2,1)S(1)} %concatenate.52, s32[5120]{0:T(1024)S(1)} %pad_clamp_fusion), kind=kCustom, calls=%fused_computation | custom fusion | bytes 18892800 | tf_op jit(solution)/shard_map/gather | solution.py:193
  221.9 8.7 fusion.73
  230.6 12.5 %all-gather.16.cloned.1.call-done = bf16[8,2,1024,128]{3,2,1,0:T(8,128)(2,1)} async-done(((bf16[8,2,128,128]{3,2,1,0:T(8,128)(2,1)}), bf16[8,2,1024,128]{3,2,1,0:T(8,128)(2,1)}) %all-gather.16.cloned.1.call-update) | async-done | bytes 4194320 | tf_op jit(solution)/shard_map/all_gather | solution.py:123
  243.1 5.0 convolution_bitcast_fusion.2
  248.1 25.3 %all-gather.18.cloned.1.call-done = bf16[8,1024,128]{2,1,0:T(8,128)(2,1)} async-done(((bf16[8,128,128]{2,1,0:T(8,128)(2,1)}), bf16[8,1024,128]{2,1,0:T(8,128)(2,1)}) %all-gather.18.cloned.1.call-update) | async-done | bytes 2097168 | tf_op jit(solution)/shard_map/all_gather | solution.py:124
  273.4 4.9 fusion.38
  278.3 5.1 fusion.2
  283.4 24.2 %scatter_custom_fusion.4 = f32[513,1024]{1,0:T(8,128)S(1)} fusion(s32[2304]{0:T(1024)S(1)} %get-tuple-element.209, f32[2304,1024]{1,0:T(8,128)} %bitcast.236, f32[]{:T(128)} %constant.43.clone.1), kind=kCustom, calls=%fused_computation.65 | custom fusion | flops 2359296 | bytes 2101760 | tf_op jit(solution)/shard_map/scatter-add | solution.py:246
  307.5 4.9 all-gather.20.cloned.1.call-done
  312.5 6.4 fusion.13
  318.9 23.9 %all-gather.22.cloned.1.call-done = bf16[8,1024,128]{2,1,0:T(8,128)(2,1)} async-done(((bf16[8,128,128]{2,1,0:T(8,128)(2,1)}), bf16[8,1024,128]{2,1,0:T(8,128)(2,1)}) %all-gather.22.cloned.1.call-update) | async-done | bytes 2097168 | tf_op jit(solution)/shard_map/all_gather | solution.py:124
  342.8 6.3 fusion.39
  349.0 5.1 fusion.7
  354.1 24.3 %scatter_fusion.1 = f32[513,1024]{1,0:T(8,128)S(1)} fusion(f32[513,1024]{1,0:T(8,128)S(1)} %scatter_custom_fusion.4, s32[2304]{0:T(1024)S(1)} %get-tuple-element.208, f32[2304,1024]{1,0:T(8,128)} %bitcast.233), kind=kCustom, calls=%fused_computation.7 | custom fusion | flops 2359296 | bytes 28320768 | tf_op jit(solution)/shard_map/scatter-add | solution.py:246
  382.9 4.3 bitcast_multiply_fusion.1
  387.2 24.2 %scatter_custom_fusion.2 = f32[513,1024]{1,0:T(8,128)S(1)} fusion(s32[2304]{0:T(1024)S(1)} %get-tuple-element.209, f32[2304,1024]{1,0:T(8,128)} %bitcast_multiply_fusion.1, f32[]{:T(128)} %constant.43.clone.1), kind=kCustom, calls=%fused_computation.67 | custom fusion | flops 2359296 | bytes 2101760 | tf_op jit(solution)/shard_map/scatter-add | solution.py:207
  411.5 3.2 fusion.80
  414.7 4.3 bitcast_multiply_fusion
  419.0 24.1 %scatter_fusion = f32[513,1024]{1,0:T(8,128)S(1)} fusion(f32[513,1024]{1,0:T(8,128)S(1)} %scatter_custom_fusion.2, s32[2304]{0:T(1024)S(1)} %get-tuple-element.208, f32[2304,1024]{1,0:T(8,128)} %bitcast_multiply_fusion), kind=kCustom, calls=%fused_computation.5 | custom fusion | flops 2359296 | bytes 28320768 | tf_op jit(solution)/shard_map/scatter-add | solution.py:207
  445.8 26.1 %reduce-scatter.16.cloned.1.call-done = bf16[128,1024]{1,0:T(8,128)(2,1)} async-done(((bf16[512,1024]{1,0:T(8,128)(2,1)}), bf16[128,1024]{1,0:T(8,128)(2,1)}) %reduce-scatter.16.cloned.1.call-update) | async-done | bytes 262160 | tf_op jit(solution)/shard_map/reduce_scatter | solution.py:209
  474.5 26.4 %all-gather.26.cloned.1.call-done = bf16[512,1024]{1,0:T(8,128)(2,1)} async-done(((bf16[128,1024]{1,0:T(8,128)(2,1)}), bf16[512,1024]{1,0:T(8,128)(2,1)}) %all-gather.26.cloned.1.call-update) | async-done | bytes 1048592 | tf_op jit(solution)/shard_map/all_gather | solution.py:264
  511.9 6.3 fusion.82
  519.2 6.4 fusion.83
  528.4 10.1 %reduce-scatter.20.cloned.1.call-done = bf16[128,1024]{1,0:T(8,128)(2,1)} async-done(((bf16[512,1024]{1,0:T(8,128)(2,1)}), bf16[128,1024]{1,0:T(8,128)(2,1)}) %reduce-scatter.20.cloned.1.call-update) | async-done | bytes 262160 | tf_op jit(solution)/shard_map/reduce_scatter | solution.py:288
  543.5 8.6 convolution_bitcast_fusion.1
  553.5 8.1 convolution_bitcast_fusion
  573.0 18.4 %reduce-scatter.30.cloned.1.call-done = f32[8,128,128]{2,1,0:T(8,128)} async-done(((f32[8,1024,128]{2,1,0:T(8,128)}), f32[8,128,128]{2,1,0:T(8,128)}) %reduce-scatter.30.cloned.1.call-update) | async-done | bytes 524304 | tf_op jit(solution)/shard_map/reduce_scatter | solution.py:249
  592.4 53.3 %reduce-scatter.32.cloned.1.call-done = f32[8,128,128]{2,1,0:T(8,128)} async-done(((f32[8,1024,128]{2,1,0:T(8,128)}), f32[8,128,128]{2,1,0:T(8,128)}) %reduce-scatter.32.cloned.1.call-update) | async-done | bytes 524304 | tf_op jit(solution)/shard_map/reduce_scatter | solution.py:249
  646.8 4.1 multiply_subtract_fusion.1
  651.0 34.3 %reduce-scatter.24.cloned.1.call-done = f32[2,128,128]{1,2,0:T(8,128)} async-done(((f32[2,1024,128]{1,2,0:T(8,128)}), f32[2,128,128]{1,2,0:T(8,128)}) %reduce-scatter.24.cloned.1.call-update) | async-done | bytes 131088 | tf_op jit(solution)/shard_map/reduce_scatter | solution.py:306
  692.6 29.8 %reduce-scatter.34.cloned.1.call-done = f32[128,2]{1,0:T(8,128)} async-done(((f32[1024,2]{1,0:T(8,128)}), f32[128,2]{1,0:T(8,128)}) %reduce-scatter.34.cloned.1.call-update) | async-done | bytes 1040
  723.3 11.7 %psum.7 = f32[2,128]{1,0:T(2,128)S(1)} all-reduce(f32[2,128]{1,0:T(2,128)S(1)} %copy.266), channel_id=1, replica_groups=mesh['dp'=8,'tensor'=4] {'tensor'}, use_global_device_ids=true, to_apply=%region_23.24 | all-reduce | flops 256 | bytes 2048 | tf_op jit(solution)/shard_map/psum | solution.py:308
  735.6 31.7 %reduce-scatter.22.cloned.1.call-done = f32[4,128,128]{1,2,0:T(8,128)} async-done(((f32[4,1024,128]{1,2,0:T(8,128)}), f32[4,128,128]{1,2,0:T(8,128)}) %reduce-scatter.22.cloned.1.call-update) | async-done | bytes 262160 | tf_op jit(solution)/shard_map/reduce_scatter | solution.py:305
  771.8 70.2 %reduce-scatter.26.cloned.1.call-done = f32[8,2,128,128]{2,3,1,0:T(8,128)} async-done(((f32[8,2,1024,128]{2,3,1,0:T(8,128)}), f32[8,2,128,128]{2,3,1,0:T(8,128)}) %reduce-scatter.26.cloned.1.call-update) | async-done | bytes 1048592 | tf_op jit(solution)/shard_map/reduce_scatter | solution.py:248
  843.4 73.3 %reduce-scatter.28.cloned.1.call-done = f32[8,2,128,128]{2,3,1,0:T(8,128)} async-done(((f32[8,2,1024,128]{2,3,1,0:T(8,128)}), f32[8,2,128,128]{2,3,1,0:T(8,128)}) %reduce-scatter.28.cloned.1.call-update) | async-done | bytes 1048592 | tf_op jit(solution)/shard_map/reduce_scatter | solution.py:248
  919.8 6.7 multiply_subtract_fusion
  929.4 3.0 copy.243
  (309 shorter events, 97.1 us)
Async XLA Ops:
  7.2 16.6 %copy-start.51 = (f32[2,128,128]{2,1,0:T(8,128)S(1)}, f32[2,128,128]{2,1,0:T(8,128)}, u32[]{:S(2)}) copy-start(f32[2,128,128]{2,1,0:T(8,128)} %param.25) | copy-start | bytes 393220
  7.2 43.1 %all-gather.10.cloned.1.call-start = ((), (), s32[]{:S(2)}) async-start(), calls=%async_computation.11 | async-start | bytes 1310720 | tf_op jit(solution)/shard_map/all_gather | solution.py:174
  18.2 113.1 %copy-start.63 = (f32[1,1024]{1,0:T(1,128)}, f32[1,1024]{1,0:T(1,128)S(1)}, u32[]{:S(2)}) copy-start(f32[1,1024]{1,0:T(1,128)S(1)} %get-tuple-element.210) | copy-start | bytes 12292
  21.8 53.8 %all-gather.12.cloned.1.call-start = ((), (), s32[]{:S(2)}) async-start(), calls=%async_computation.12 | async-start | bytes 1179648 | tf_op jit(solution)/shard_map/all_gather | solution.py:162
  23.7 105.9 %reduce-scatter.14.cloned.1.call-start = ((), (), s32[]{:S(2)}) async-start(), calls=%async_computation.13 | async-start | bytes 2621440 | tf_op jit(solution)/shard_map/reduce_scatter | solution.py:187
  33.7 49.6 %copy-start.13 = (bf16[2,1024,128]{2,1,0:T(8,128)(2,1)}, bf16[2,1024,128]{2,1,0:T(8,128)(2,1)S(1)}, u32[]{:S(2)}) copy-start(bf16[2,1024,128]{2,1,0:T(8,128)(2,1)S(1)} %all_gather.40) | copy-start | bytes 1572868
  33.7 46.4 %copy-start.19 = (pred[512,512]{0,1:T(8,128)(4,1)}, pred[512,512]{0,1:T(8,128)(4,1)S(1)}, u32[]{:S(2)}) copy-start(pred[512,512]{0,1:T(8,128)(4,1)S(1)} %iota_compare_fusion) | copy-start | bytes 786436
  34.1 44.0 %copy-start.38 = (f32[512,32]{0,1:T(8,128)}, f32[512,32]{0,1:T(8,128)S(1)}, u32[]{:S(2)}) copy-start(f32[512,32]{0,1:T(8,128)S(1)} %get-tuple-element.216) | copy-start | bytes 196612
  34.1 44.0 %copy-start.40 = (f32[512,32]{0,1:T(8,128)}, f32[512,32]{0,1:T(8,128)S(1)}, u32[]{:S(2)}) copy-start(f32[512,32]{0,1:T(8,128)S(1)} %get-tuple-element.217) | copy-start | bytes 196612
  84.0 45.6 %copy-start.3 = (f32[128,1024]{1,0:T(8,128)S(1)}, f32[128,1024]{1,0:T(8,128)}, u32[]{:S(2)}) copy-start(f32[128,1024]{1,0:T(8,128)} %param.19) | copy-start | bytes 1572868
  85.8 47.0 %copy-start.9 = (f32[16,2,128,128]{3,2,1,0:T(8,128)S(1)}, f32[16,2,128,128]{3,2,1,0:T(8,128)}, u32[]{:S(2)}) copy-start(f32[16,2,128,128]{3,2,1,0:T(8,128)} %param.26) | copy-start | bytes 6291460
  85.8 90.1 %all-gather.24.cloned.1.call-start = ((), (), s32[]{:S(2)}) async-start(), calls=%async_computation.20 | async-start | bytes 2621440 | tf_op jit(solution)/shard_map/all_gather | solution.py:212
  86.4 119.2 %all-gather.14.cloned.1.call-start = ((), (), s32[]{:S(2)}) async-start(), calls=%async_computation.14 | async-start | bytes 1310720 | tf_op jit(solution)/shard_map/all_gather | solution.py:190
  132.7 110.4 %all-gather.16.cloned.1.call-start = ((), (), s32[]{:S(2)}) async-start(), calls=%async_computation.15 | async-start | bytes 4718592 | tf_op jit(solution)/shard_map/all_gather | solution.py:123
  134.0 139.4 %all-gather.18.cloned.1.call-start = ((), (), s32[]{:S(2)}) async-start(), calls=%async_computation.16 | async-start | bytes 2359296 | tf_op jit(solution)/shard_map/all_gather | solution.py:124
  135.4 20.2 %copy-start.67 = (f32[512,8]{0,1:T(8,128)S(1)}, f32[512,8]{0,1:T(8,128)}, u32[]{:S(2)}) copy-start(f32[512,8]{0,1:T(8,128)} %param.22) | copy-start | bytes 49156
  136.2 176.2 %all-gather.20.cloned.1.call-start = ((), (), s32[]{:S(2)}) async-start(), calls=%async_computation.17 | async-start | bytes 4718592 | tf_op jit(solution)/shard_map/all_gather | solution.py:123
  137.0 205.8 %all-gather.22.cloned.1.call-start = ((), (), s32[]{:S(2)}) async-start(), calls=%async_computation.18 | async-start | bytes 2359296 | tf_op jit(solution)/shard_map/all_gather | solution.py:124
  137.7 306.7 %reduce-scatter.18.cloned.1.call-start = ((), (), s32[]{:S(2)}) async-start(), calls=%async_computation.21 | async-start | bytes 2621440 | tf_op jit(solution)/shard_map/reduce_scatter | solution.py:255
  278.3 5.1 copy-start.25
  278.3 5.1 copy-start.27
  342.8 6.3 copy-start.5
  379.9 91.9 %reduce-scatter.16.cloned.1.call-start = ((), (), s32[]{:S(2)}) async-start(), calls=%async_computation.19 | async-start | bytes 1310720 | tf_op jit(solution)/shard_map/reduce_scatter | solution.py:209
  443.2 28.7 %copy-start.76 = (f32[128]{0:T(128)S(1)}, f32[128]{0:T(128)}, u32[]{:S(2)}) copy-start(f32[128]{0:T(128)} %get-tuple-element.214) | copy-start | bytes 1540
  444.3 27.5 %copy-start.35 = (f32[128,1024]{1,0:T(8,128)S(1)}, f32[128,1024]{1,0:T(8,128)}, u32[]{:S(2)}) copy-start(f32[128,1024]{1,0:T(8,128)} %param.20) | copy-start | bytes 1572868
  444.3 29.9 %copy-start.14 = (bf16[2,1024,128]{2,1,0:T(8,128)(2,1)S(1)}, bf16[2,1024,128]{2,1,0:T(8,128)(2,1)}, u32[]{:S(2)}) copy-start(bf16[2,1024,128]{2,1,0:T(8,128)(2,1)} %copy-done.13) | copy-start | bytes 1572868
  444.4 56.5 %all-gather.26.cloned.1.call-start = ((), (), s32[]{:S(2)}) async-start(), calls=%async_computation.22 | async-start | bytes 1310720 | tf_op jit(solution)/shard_map/all_gather | solution.py:264
  474.2 64.3 %reduce-scatter.20.cloned.1.call-start = ((), (), s32[]{:S(2)}) async-start(), calls=%async_computation.23 | async-start | bytes 1310720 | tf_op jit(solution)/shard_map/reduce_scatter | solution.py:288
  474.5 28.2 %copy-start.12 = (bf16[2,2,512,512]{2,3,0,1:T(8,128)(2,1)S(1)}, bf16[2,2,512,512]{2,3,0,1:T(8,128)(2,1)}, u32[]{:S(2)}) copy-start(bf16[2,2,512,512]{2,3,0,1:T(8,128)(2,1)} %copy-done.11) | copy-start | bytes 6291460
  511.7 79.7 %reduce-scatter.30.cloned.1.call-start = ((), (), s32[]{:S(2)}) async-start(), calls=%async_computation.28 | async-start | bytes 4718592 | tf_op jit(solution)/shard_map/reduce_scatter | solution.py:249
  518.2 127.5 %reduce-scatter.32.cloned.1.call-start = ((), (), s32[]{:S(2)}) async-start(), calls=%async_computation.29 | async-start | bytes 4718592 | tf_op jit(solution)/shard_map/reduce_scatter | solution.py:249
  525.7 12.9 %copy-start.4 = (f32[128,1024]{1,0:T(8,128)S(1)}, f32[128,1024]{1,0:T(8,128)}, u32[]{:S(2)}) copy-start(f32[128,1024]{1,0:T(8,128)} %param.19) | copy-start | bytes 1572868
  525.7 12.8 %copy-start.62 = (f32[1,1024]{1,0:T(1,128)S(1)}, f32[1,1024]{1,0:T(1,128)}, u32[]{:S(2)}) copy-start(f32[1,1024]{1,0:T(1,128)} %copy-done.61) | copy-start | bytes 12292
  525.7 12.8 %copy-start.71 = (f32[128]{0:T(128)S(1)}, f32[128]{0:T(128)}, u32[]{:S(2)}) copy-start(f32[128]{0:T(128)} %copy-done.70) | copy-start | bytes 1540
  525.7 15.6 %copy-start.42 = (bf16[512,1024]{1,0:T(8,128)(2,1)S(1)}, bf16[512,1024]{1,0:T(8,128)(2,1)}, u32[]{:S(2)}) copy-start(bf16[512,1024]{1,0:T(8,128)(2,1)} %all-gather.10.cloned.1.call-done) | copy-start | bytes 3145732
  525.7 159.6 %reduce-scatter.24.cloned.1.call-start = ((), (), s32[]{:S(2)}) async-start(), calls=%async_computation.25 | async-start | bytes 1179648 | tf_op jit(solution)/shard_map/reduce_scatter | solution.py:306
  528.3 194.0 %reduce-scatter.34.cloned.1.call-start = ((), (), s32[]{:S(2)}) async-start(), calls=%async_computation.30 | async-start | bytes 589824
  541.3 226.0 %reduce-scatter.22.cloned.1.call-start = ((), (), s32[]{:S(2)}) async-start(), calls=%async_computation.24 | async-start | bytes 2359296 | tf_op jit(solution)/shard_map/reduce_scatter | solution.py:305
  543.4 298.6 %reduce-scatter.26.cloned.1.call-start = ((), (), s32[]{:S(2)}) async-start(), calls=%async_computation.26 | async-start | bytes 9437184 | tf_op jit(solution)/shard_map/reduce_scatter | solution.py:248
  552.1 364.6 %reduce-scatter.28.cloned.1.call-start = ((), (), s32[]{:S(2)}) async-start(), calls=%async_computation.27 | async-start | bytes 9437184 | tf_op jit(solution)/shard_map/reduce_scatter | solution.py:248
  570.0 76.8 %copy-start.15 = (f32[16,128,128]{2,1,0:T(8,128)S(1)}, f32[16,128,128]{2,1,0:T(8,128)}, u32[]{:S(2)}) copy-start(f32[16,128,128]{2,1,0:T(8,128)} %param.27) | copy-start | bytes 3145732
  650.9 40.0 %copy-start.36 = (f32[128,1024]{1,0:T(8,128)S(1)}, f32[128,1024]{1,0:T(8,128)}, u32[]{:S(2)}) copy-start(f32[128,1024]{1,0:T(8,128)} %get-tuple-element.178) | copy-start | bytes 1572868
  650.9 40.0 %copy-start.44 = (bf16[128,1024]{1,0:T(8,128)(2,1)S(1)}, bf16[128,1024]{1,0:T(8,128)(2,1)}, u32[]{:S(2)}) copy-start(bf16[128,1024]{1,0:T(8,128)(2,1)} %reduce-scatter.20.cloned.1.call-done) | copy-start | bytes 786436
  650.9 84.0 %copy-start.73 = (f32[2,128]{1,0:T(2,128)S(1)}, f32[2,128]{1,0:T(2,128)}, u32[]{:S(2)}) copy-start(f32[2,128]{1,0:T(2,128)} %param.23) | copy-start | bytes 3076
  651.0 84.0 %copy-start.74 = (f32[2,128]{1,0:T(2,128)S(1)}, f32[2,128]{1,0:T(2,128)}, u32[]{:S(2)}) copy-start(f32[2,128]{1,0:T(2,128)} %param.28) | copy-start | bytes 3076
  651.0 116.3 %copy-start.24 = (f32[4,128,128]{1,2,0:T(8,128)S(1)}, f32[4,128,128]{1,2,0:T(8,128)}, u32[]{:S(2)}) copy-start(f32[4,128,128]{1,2,0:T(8,128)} %copy-done.23) | copy-start | bytes 786436
  685.3 49.7 %copy-start.75 = (f32[2,128]{1,0:T(2,128)S(1)}, f32[2,128]{1,0:T(2,128)}, u32[]{:S(2)}) copy-start(f32[2,128]{1,0:T(2,128)} %param.29) | copy-start | bytes 3076
  735.0 108.4 %copy-start.72 = (f32[2,128]{1,0:T(2,128)}, f32[2,128]{1,0:T(2,128)S(1)}, u32[]{:S(2)}) copy-start(f32[2,128]{1,0:T(2,128)S(1)} %psum.7) | copy-start | bytes 3076
  (49 other events, 91.7 us)
Sparse Core Ops, SparseCore 0:
  21.9 28.2 all-gather.9
  52.7 22.8 all-gather.11
  85.9 43.6 reduce-scatter.13
  131.0 44.8 all-gather.23
  177.9 26.7 all-gather.13
  207.1 35.9 all-gather.15
  245.6 27.7 all-gather.17
  275.9 36.5 all-gather.19
  315.0 27.7 all-gather.21
  380.1 43.5 reduce-scatter.17
  444.5 27.3 reduce-scatter.15
  474.4 26.4 all-gather.25
  511.8 26.6 reduce-scatter.19
  541.7 49.5 reduce-scatter.29
  594.6 51.0 reduce-scatter.31
  649.3 35.9 reduce-scatter.23
  688.2 34.0 reduce-scatter.33
  726.1 41.1 reduce-scatter.21
  770.7 71.2 reduce-scatter.25
  845.3 71.2 reduce-scatter.27
where the time goes:
time: 950 us; the launch traced here: 941 us
  waiting for transfers between devices  531 us (56%)
  other arithmetic  148 us (16%)
  local copies, waits for them, and re-layouts  130 us (14%)
  matrix products  83.7 us (9%)
  blocking collectives  31.8 us (3%)
  between operations  15.7 us (2%)
    reduce_scatter x2, waiting for transfers between devices, local(): lax.psum_scatter(gate_up_local, 'dp', scatter_dimension=2, tiled=True)  144 us
    reduce_scatter x2, waiting for transfers between devices, local(): lax.psum_scatter(down_local, 'dp', scatter_dimension=1, tiled=True)  71.7 us
    all_gather x2, waiting for transfers between devices, fetch_experts(): lax.all_gather(down_part, 'dp', axis=1, tiled=True)  49.2 us
    scatter-add x2, other arithmetic, local(): back_sum = back_sum.at[slot_rows].add(input_cot.reshape(-1, width))  48.5 us
    scatter-add x2, other arithmetic, local(): mixture.at[slot_rows]  48.4 us
    unnamed x180, local copies, waits for them, and re-layouts  43.3 us
    reduce_scatter x1, waiting for transfers between devices, local(): lax.psum_scatter(partial_value, 'tensor', scatter_dimension=0, tiled=True)  43.2 us
    reduce_scatter x1, waiting for transfers between devices, local(): lax.psum_scatter(out_local, 'dp', scatter_dimension=1, tiled=True)  34.3 us
  transfers between devices with their start and end apart: 20, of which 18 were waited for; matrix products, arithmetic and copies ran while one was open for 29% of the time, Pallas kernels for 0%

commit v1 on v0

--- a/solution.py
+++ b/solution.py
@@ -16,6 +16,15 @@
 rate_gain = 0.2
 decay_matrix = 0.1
 rope_base = 10000.0
+place_shards_all = lambda sample, bus_axis: jnp.concatenate(
+    jax.lax.all_to_all(
+        jnp.stack([sample for _ in range(jax.lax.axis_size(bus_axis))], axis=0),
+        axis_name=bus_axis,
+        split_axis=0,
+        concat_axis=0,
+    ),
+    axis=1,
+)
 
 
 def rope_tables(length, width):
@@ -121,7 +130,7 @@
     down_part = w_down[start_expert : start_expert + per_turn].astype(jnp.bfloat16)
     return (
         lax.all_gather(gate_up_part, "dp", axis=2, tiled=True),
-        lax.all_gather(down_part, "dp", axis=1, tiled=True),
+        place_shards_all(down_part, "dp"),
     )
 
 

time: 950 us -> 916 us (0.964)
  waiting for transfers between devices: 531 us -> 484 us
    all_gather x2 -> x0, waiting for transfers between devices: 49.2 us -> none  [fetch_experts(): lax.all_gather(down_part, 'dp', axis=1, tiled=True)]
    all_to_all x0 -> x2, waiting for transfers between devices: none -> 24.4 us  [jax.lax.all_to_all(jnp.stack([sample for _ in range(jax.lax.axis_size(bus...]
    all_gather x2, waiting for transfers between devices: 17.5 us -> 0.02 us  [fetch_experts(): lax.all_gather(gate_up_part, 'dp', axis=2, tiled=True)]
    unnamed x180 -> x186, local copies, waits for them, and re-layouts: 43.3 us -> 44.2 us
    unnamed x21 -> x19, waiting for transfers between devices: 32 us -> 31.3 us
  transfers between devices with their start and end apart: 20 -> 20, of which waited for: 18 -> 14; matrix products, arithmetic and copies ran while one was open for 29% -> 30% of each run, Pallas kernels for 0% -> 0%
where the time goes in v1:
time: 916 us; the launch traced here: 906 us
  waiting for transfers between devices  484 us (53%)
  other arithmetic  148 us (16%)
  local copies, waits for them, and re-layouts  138 us (15%)
  matrix products  79.1 us (9%)
  blocking collectives  31.8 us (3%)
  between operations  15.8 us (2%)
  starting transfers between devices  9.39 us (1%)
    reduce_scatter x2, waiting for transfers between devices, local(): lax.psum_scatter(gate_up_local, 'dp', scatter_dimension=2, tiled=True)  143 us
    reduce_scatter x2, waiting for transfers between devices, local(): lax.psum_scatter(down_local, 'dp', scatter_dimension=1, tiled=True)  71.8 us
    scatter-add x2, other arithmetic, local(): back_sum = back_sum.at[slot_rows].add(input_cot.reshape(-1, width))  48.4 us
    scatter-add x2, other arithmetic, local(): mixture.at[slot_rows]  48.4 us
    unnamed x186, local copies, waits for them, and re-layouts  44.2 us
    reduce_scatter x1, waiting for transfers between devices, local(): lax.psum_scatter(partial_value, 'tensor', scatter_dimension=0, tiled=True)  43.2 us
    reduce_scatter x1, waiting for transfers between devices, local(): lax.psum_scatter(out_local, 'dp', scatter_dimension=1, tiled=True)  34.3 us
    reduce_scatter x1, waiting for transfers between devices, local(): lax.psum_scatter(attn_local, 'dp', scatter_dimension=1, tiled=True)  31.6 us
  transfers between devices with their start and end apart: 20, of which 14 were waited for; matrix products, arithmetic and copies ran while one was open for 30% of the time, Pallas kernels for 0%

profile of v1, /device:TPU:0, one launch (start us, length us, event | category | flops | bytes accessed | tf_op | source)
XLA Modules:
  0.0 906.2 jit_solution(16293254791257228627)
XLA Ops:
  8.0 10.3 %all_gather.29 = bf16[2,1024]{1,0:T(2,128)(2,1)S(1)} all-gather(bf16[2,128]{1,0:T(2,128)(2,1)S(1)} %convert_element_type.103), channel_id=1, replica_groups=mesh['dp'=8,'tensor'=4] {'dp'}, dimensions={1}, use_global_device_ids=true | all-gather | bytes 4608 | tf_op jit(solution)/shard_map/all_gather | solution.py:170
  23.8 9.8 %all_gather.32 = bf16[2,1024,128]{2,1,0:T(8,128)(2,1)S(1)} all-gather(bf16[2,128,128]{2,1,0:T(8,128)(2,1)S(1)} %convert_element_type.110), channel_id=1, replica_groups=mesh['dp'=8,'tensor'=4] {'dp'}, dimensions={1}, use_global_device_ids=true | all-gather | bytes 589824 | tf_op jit(solution)/shard_map/all_gather | solution.py:172
  34.1 16.1 %all-gather.8.cloned.1.call-done = bf16[512,1024]{1,0:T(8,128)(2,1)} async-done(((bf16[128,1024]{1,0:T(8,128)(2,1)}), bf16[512,1024]{1,0:T(8,128)(2,1)}) %all-gather.8.cloned.1.call-update) | async-done | bytes 1048592 | tf_op jit(solution)/shard_map/all_gather | solution.py:183
  50.3 25.3 %all-gather.10.cloned.1.call-done = bf16[4,1024,128]{1,2,0:T(8,128)(2,1)} async-done(((bf16[4,128,128]{1,2,0:T(8,128)(2,1)}), bf16[4,1024,128]{1,2,0:T(8,128)(2,1)}) %all-gather.10.cloned.1.call-update) | async-done | bytes 1048592 | tf_op jit(solution)/shard_map/all_gather | solution.py:171
  86.5 43.2 %reduce-scatter.14.cloned.1.call-done = f32[128,1024]{1,0:T(8,128)} async-done(((f32[512,1024]{1,0:T(8,128)}), f32[128,1024]{1,0:T(8,128)}) %reduce-scatter.14.cloned.1.call-update) | async-done | bytes 524304 | tf_op jit(solution)/shard_map/reduce_scatter | solution.py:196
  137.2 3.8 all-to-all-start
  143.2 24.4 %all-to-all-done = bf16[8,8,128,128]{3,2,1,0:T(8,128)(2,1)S(1)} async-done(((bf16[8,8,128,128]{3,2,1,0:T(8,128)(2,1)}), bf16[8,8,128,128]{3,2,1,0:T(8,128)(2,1)S(1)}, u32[]{:S(2)}, u32[]{:S(2)}) %all-to-all-start) | async-done | bytes 2097184 | tf_op jit(solution)/shard_map/all_to_all | solution.py:20
  169.5 4.5 all-to-all-start.1
  175.0 15.5 %scatter_custom_fusion = s32[4608]{0:T(1024)S(1)} fusion(s32[4096]{0:T(1024)S(1)} %bitcast.280, s32[4096]{0:T(1024)S(1)} %reshape.373, s32[]{:T(128)} %constant.51.clone.1), kind=kCustom, calls=%fused_computation.145 | custom fusion | bytes 18436 | tf_op jit(solution)/shard_map/scatter | solution.py:123
  190.5 16.0 %scatter_custom_fusion.1 = f32[4608]{0:T(1024)S(1)} fusion(s32[4096]{0:T(1024)S(1)} %bitcast.281, f32[4096]{0:T(1024)S(1)} %reshape.381, f32[]{:T(128)} %constant.43.clone.1), kind=kCustom, calls=%fused_computation.143 | custom fusion | bytes 18436 | tf_op jit(solution)/shard_map/scatter | solution.py:124
  208.0 3.2 copy.209
  212.9 15.2 %gather_fusion.1 = f32[4608,1024]{1,0:T(8,128)} fusion(f32[513,1024]{1,0:T(8,128)S(1)} %concatenate.53, s32[5120]{0:T(1024)S(1)} %pad_clamp_fusion), kind=kCustom, calls=%fused_computation.1 | custom fusion | bytes 37767168 | tf_op jit(solution)/shard_map/gather | solution.py:224
  228.1 8.0 multiply_convert_fusion
  236.1 4.8 fusion.72
  242.3 14.9 %gather_fusion = bf16[4608,1024]{1,0:T(8,128)(2,1)} fusion(bf16[513,1024]{1,0:T(8,128)(2,1)S(1)} %concatenate.52, s32[5120]{0:T(1024)S(1)} %pad_clamp_fusion), kind=kCustom, calls=%fused_computation | custom fusion | bytes 18892800 | tf_op jit(solution)/shard_map/gather | solution.py:202
  257.2 8.5 fusion.73
  265.7 5.8 convolution_bitcast_fusion.2
  274.3 5.1 fusion.2
  279.4 24.0 %scatter_custom_fusion.4 = f32[513,1024]{1,0:T(8,128)S(1)} fusion(s32[2304]{0:T(1024)S(1)} %get-tuple-element.209, f32[2304,1024]{1,0:T(8,128)} %bitcast.240, f32[]{:T(128)} %constant.43.clone.1), kind=kCustom, calls=%fused_computation.65 | custom fusion | flops 2359296 | bytes 2101760 | tf_op jit(solution)/shard_map/scatter-add | solution.py:255
  303.5 5.1 fusion.13
  308.7 5.1 fusion.39
  313.8 5.1 fusion.7
  318.9 24.3 %scatter_fusion.1 = f32[513,1024]{1,0:T(8,128)S(1)} fusion(f32[513,1024]{1,0:T(8,128)S(1)} %scatter_custom_fusion.4, s32[2304]{0:T(1024)S(1)} %get-tuple-element.208, f32[2304,1024]{1,0:T(8,128)} %bitcast.237), kind=kCustom, calls=%fused_computation.7 | custom fusion | flops 2359296 | bytes 28320768 | tf_op jit(solution)/shard_map/scatter-add | solution.py:255
  347.7 4.3 bitcast_multiply_fusion.1
  352.0 24.2 %scatter_custom_fusion.2 = f32[513,1024]{1,0:T(8,128)S(1)} fusion(s32[2304]{0:T(1024)S(1)} %get-tuple-element.209, f32[2304,1024]{1,0:T(8,128)} %bitcast_multiply_fusion.1, f32[]{:T(128)} %constant.43.clone.1), kind=kCustom, calls=%fused_computation.67 | custom fusion | flops 2359296 | bytes 2101760 | tf_op jit(solution)/shard_map/scatter-add | solution.py:216
  376.2 3.2 fusion.80
  379.4 4.3 bitcast_multiply_fusion
  383.8 24.1 %scatter_fusion = f32[513,1024]{1,0:T(8,128)S(1)} fusion(f32[513,1024]{1,0:T(8,128)S(1)} %scatter_custom_fusion.2, s32[2304]{0:T(1024)S(1)} %get-tuple-element.208, f32[2304,1024]{1,0:T(8,128)} %bitcast_multiply_fusion), kind=kCustom, calls=%fused_computation.5 | custom fusion | flops 2359296 | bytes 28320768 | tf_op jit(solution)/shard_map/scatter-add | solution.py:216
  410.5 26.3 %reduce-scatter.16.cloned.1.call-done = bf16[128,1024]{1,0:T(8,128)(2,1)} async-done(((bf16[512,1024]{1,0:T(8,128)(2,1)}), bf16[128,1024]{1,0:T(8,128)(2,1)}) %reduce-scatter.16.cloned.1.call-update) | async-done | bytes 262160 | tf_op jit(solution)/shard_map/reduce_scatter | solution.py:218
  439.5 26.3 %all-gather.20.cloned.1.call-done = bf16[512,1024]{1,0:T(8,128)(2,1)} async-done(((bf16[128,1024]{1,0:T(8,128)(2,1)}), bf16[512,1024]{1,0:T(8,128)(2,1)}) %all-gather.20.cloned.1.call-update) | async-done | bytes 1048592 | tf_op jit(solution)/shard_map/all_gather | solution.py:273
  473.7 2.9 bitcast_convert_fusion
  476.9 6.3 fusion.82
  484.2 6.4 fusion.83
  493.4 10.1 %reduce-scatter.20.cloned.1.call-done = bf16[128,1024]{1,0:T(8,128)(2,1)} async-done(((bf16[512,1024]{1,0:T(8,128)(2,1)}), bf16[128,1024]{1,0:T(8,128)(2,1)}) %reduce-scatter.20.cloned.1.call-update) | async-done | bytes 262160 | tf_op jit(solution)/shard_map/reduce_scatter | solution.py:297
  508.4 8.6 convolution_bitcast_fusion.1
  518.4 8.1 convolution_bitcast_fusion
  534.9 3.0 copy.234
  537.9 18.4 %reduce-scatter.30.cloned.1.call-done = f32[8,128,128]{2,1,0:T(8,128)} async-done(((f32[8,1024,128]{2,1,0:T(8,128)}), f32[8,128,128]{2,1,0:T(8,128)}) %reduce-scatter.30.cloned.1.call-update) | async-done | bytes 524304 | tf_op jit(solution)/shard_map/reduce_scatter | solution.py:258
  557.4 53.4 %reduce-scatter.32.cloned.1.call-done = f32[8,128,128]{2,1,0:T(8,128)} async-done(((f32[8,1024,128]{2,1,0:T(8,128)}), f32[8,128,128]{2,1,0:T(8,128)}) %reduce-scatter.32.cloned.1.call-update) | async-done | bytes 524304 | tf_op jit(solution)/shard_map/reduce_scatter | solution.py:258
  611.9 4.1 multiply_subtract_fusion.1
  616.0 34.3 %reduce-scatter.24.cloned.1.call-done = f32[2,128,128]{1,2,0:T(8,128)} async-done(((f32[2,1024,128]{1,2,0:T(8,128)}), f32[2,128,128]{1,2,0:T(8,128)}) %reduce-scatter.24.cloned.1.call-update) | async-done | bytes 131088 | tf_op jit(solution)/shard_map/reduce_scatter | solution.py:315
  657.6 29.8 %reduce-scatter.34.cloned.1.call-done = f32[128,2]{1,0:T(8,128)} async-done(((f32[1024,2]{1,0:T(8,128)}), f32[128,2]{1,0:T(8,128)}) %reduce-scatter.34.cloned.1.call-update) | async-done | bytes 1040
  688.3 11.7 %psum.7 = f32[2,128]{1,0:T(2,128)S(1)} all-reduce(f32[2,128]{1,0:T(2,128)S(1)} %copy.270), channel_id=1, replica_groups=mesh['dp'=8,'tensor'=4] {'tensor'}, use_global_device_ids=true, to_apply=%region_23.24 | all-reduce | flops 256 | bytes 2048 | tf_op jit(solution)/shard_map/psum | solution.py:317
  700.6 31.6 %reduce-scatter.22.cloned.1.call-done = f32[4,128,128]{1,2,0:T(8,128)} async-done(((f32[4,1024,128]{1,2,0:T(8,128)}), f32[4,128,128]{1,2,0:T(8,128)}) %reduce-scatter.22.cloned.1.call-update) | async-done | bytes 262160 | tf_op jit(solution)/shard_map/reduce_scatter | solution.py:314
  736.9 70.0 %reduce-scatter.26.cloned.1.call-done = f32[8,2,128,128]{2,3,1,0:T(8,128)} async-done(((f32[8,2,1024,128]{2,3,1,0:T(8,128)}), f32[8,2,128,128]{2,3,1,0:T(8,128)}) %reduce-scatter.26.cloned.1.call-update) | async-done | bytes 1048592 | tf_op jit(solution)/shard_map/reduce_scatter | solution.py:257
  808.2 73.3 %reduce-scatter.28.cloned.1.call-done = f32[8,2,128,128]{2,3,1,0:T(8,128)} async-done(((f32[8,2,1024,128]{2,3,1,0:T(8,128)}), f32[8,2,128,128]{2,3,1,0:T(8,128)}) %reduce-scatter.28.cloned.1.call-update) | async-done | bytes 1048592 | tf_op jit(solution)/shard_map/reduce_scatter | solution.py:257
  884.7 6.7 multiply_subtract_fusion
  894.3 3.0 copy.247
  (317 shorter events, 97.5 us)
Async XLA Ops:
  7.2 16.6 %copy-start.54 = (f32[2,128,128]{2,1,0:T(8,128)S(1)}, f32[2,128,128]{2,1,0:T(8,128)}, u32[]{:S(2)}) copy-start(f32[2,128,128]{2,1,0:T(8,128)} %param.25) | copy-start | bytes 393220
  7.2 43.1 %all-gather.8.cloned.1.call-start = ((), (), s32[]{:S(2)}) async-start(), calls=%async_computation.13 | async-start | bytes 1310720 | tf_op jit(solution)/shard_map/all_gather | solution.py:183
  18.2 113.2 %copy-start.66 = (f32[1,1024]{1,0:T(1,128)}, f32[1,1024]{1,0:T(1,128)S(1)}, u32[]{:S(2)}) copy-start(f32[1,1024]{1,0:T(1,128)S(1)} %get-tuple-element.210) | copy-start | bytes 12292
  21.8 53.8 %all-gather.10.cloned.1.call-start = ((), (), s32[]{:S(2)}) async-start(), calls=%async_computation.14 | async-start | bytes 1179648 | tf_op jit(solution)/shard_map/all_gather | solution.py:171
  23.7 105.9 %reduce-scatter.14.cloned.1.call-start = ((), (), s32[]{:S(2)}) async-start(), calls=%async_computation.15 | async-start | bytes 2621440 | tf_op jit(solution)/shard_map/reduce_scatter | solution.py:196
  33.7 49.6 %copy-start.17 = (bf16[2,1024,128]{2,1,0:T(8,128)(2,1)}, bf16[2,1024,128]{2,1,0:T(8,128)(2,1)S(1)}, u32[]{:S(2)}) copy-start(bf16[2,1024,128]{2,1,0:T(8,128)(2,1)S(1)} %all_gather.32) | copy-start | bytes 1572868
  33.8 46.3 %copy-start.23 = (pred[512,512]{0,1:T(8,128)(4,1)}, pred[512,512]{0,1:T(8,128)(4,1)S(1)}, u32[]{:S(2)}) copy-start(pred[512,512]{0,1:T(8,128)(4,1)S(1)} %iota_compare_fusion) | copy-start | bytes 786436
  34.1 44.0 %copy-start.41 = (f32[512,32]{0,1:T(8,128)}, f32[512,32]{0,1:T(8,128)S(1)}, u32[]{:S(2)}) copy-start(f32[512,32]{0,1:T(8,128)S(1)} %get-tuple-element.216) | copy-start | bytes 196612
  34.1 44.0 %copy-start.43 = (f32[512,32]{0,1:T(8,128)}, f32[512,32]{0,1:T(8,128)S(1)}, u32[]{:S(2)}) copy-start(f32[512,32]{0,1:T(8,128)S(1)} %get-tuple-element.217) | copy-start | bytes 196612
  84.0 45.6 %copy-start.4 = (f32[128,1024]{1,0:T(8,128)S(1)}, f32[128,1024]{1,0:T(8,128)}, u32[]{:S(2)}) copy-start(f32[128,1024]{1,0:T(8,128)} %param.19) | copy-start | bytes 1572868
  85.8 47.0 %copy-start.10 = (f32[16,2,128,128]{3,2,1,0:T(8,128)S(1)}, f32[16,2,128,128]{3,2,1,0:T(8,128)}, u32[]{:S(2)}) copy-start(f32[16,2,128,128]{3,2,1,0:T(8,128)} %param.26) | copy-start | bytes 6291460
  85.8 125.3 %all-gather.18.cloned.1.call-start = ((), (), s32[]{:S(2)}) async-start(), calls=%async_computation.20 | async-start | bytes 2621440 | tf_op jit(solution)/shard_map/all_gather | solution.py:221
  86.4 154.6 %all-gather.12.cloned.1.call-start = ((), (), s32[]{:S(2)}) async-start(), calls=%async_computation.16 | async-start | bytes 1310720 | tf_op jit(solution)/shard_map/all_gather | solution.py:199
  132.7 133.0 %all-gather.14.cloned.1.call-start = ((), (), s32[]{:S(2)}) async-start(), calls=%async_computation.17 | async-start | bytes 4718592 | tf_op jit(solution)/shard_map/all_gather | solution.py:132
  137.2 30.4 %all-to-all-start = ((bf16[8,8,128,128]{3,2,1,0:T(8,128)(2,1)}), bf16[8,8,128,128]{3,2,1,0:T(8,128)(2,1)S(1)}, u32[]{:S(2)}, u32[]{:S(2)}) async-start(bf16[8,8,128,128]{3,2,1,0:T(8,128)(2,1)} %stack.22), calls=%async_computation.1 | async-start | bytes 4194304 | tf_op jit(solution)/shard_map/all_to_all | solution.py:20
  141.0 162.5 %all-gather.16.cloned.1.call-start = ((), (), s32[]{:S(2)}) async-start(), calls=%async_computation.18 | async-start | bytes 4718592 | tf_op jit(solution)/shard_map/all_gather | solution.py:132
  169.5 38.6 %all-to-all-start.1 = ((bf16[8,8,128,128]{3,2,1,0:T(8,128)(2,1)}), bf16[8,8,128,128]{3,2,1,0:T(8,128)(2,1)}, u32[]{:S(2)}, u32[]{:S(2)}) async-start(bf16[8,8,128,128]{3,2,1,0:T(8,128)(2,1)} %stack.23), calls=%async_computation.2 | async-start | bytes 4194304 | tf_op jit(solution)/shard_map/all_to_all | solution.py:20
  173.9 235.2 %reduce-scatter.18.cloned.1.call-start = ((), (), s32[]{:S(2)}) async-start(), calls=%async_computation.21 | async-start | bytes 2621440 | tf_op jit(solution)/shard_map/reduce_scatter | solution.py:264
  265.7 5.8 copy-start.1
  265.7 6.3 copy-start.15
  273.9 5.5 copy-start.29
  273.9 5.5 copy-start.31
  344.7 92.1 %reduce-scatter.16.cloned.1.call-start = ((), (), s32[]{:S(2)}) async-start(), calls=%async_computation.19 | async-start | bytes 1310720 | tf_op jit(solution)/shard_map/reduce_scatter | solution.py:218
  407.9 28.9 %copy-start.79 = (f32[128]{0:T(128)S(1)}, f32[128]{0:T(128)}, u32[]{:S(2)}) copy-start(f32[128]{0:T(128)} %get-tuple-element.214) | copy-start | bytes 1540
  409.1 27.7 %copy-start.39 = (f32[128,1024]{1,0:T(8,128)S(1)}, f32[128,1024]{1,0:T(8,128)}, u32[]{:S(2)}) copy-start(f32[128,1024]{1,0:T(8,128)} %param.20) | copy-start | bytes 1572868
  409.1 30.1 %copy-start.18 = (bf16[2,1024,128]{2,1,0:T(8,128)(2,1)S(1)}, bf16[2,1024,128]{2,1,0:T(8,128)(2,1)}, u32[]{:S(2)}) copy-start(bf16[2,1024,128]{2,1,0:T(8,128)(2,1)} %copy-done.17) | copy-start | bytes 1572868
  409.1 56.7 %all-gather.20.cloned.1.call-start = ((), (), s32[]{:S(2)}) async-start(), calls=%async_computation.22 | async-start | bytes 1310720 | tf_op jit(solution)/shard_map/all_gather | solution.py:273
  439.2 64.3 %reduce-scatter.20.cloned.1.call-start = ((), (), s32[]{:S(2)}) async-start(), calls=%async_computation.23 | async-start | bytes 1310720 | tf_op jit(solution)/shard_map/reduce_scatter | solution.py:297
  439.5 28.2 %copy-start.13 = (bf16[2,2,512,512]{2,3,0,1:T(8,128)(2,1)S(1)}, bf16[2,2,512,512]{2,3,0,1:T(8,128)(2,1)}, u32[]{:S(2)}) copy-start(bf16[2,2,512,512]{2,3,0,1:T(8,128)(2,1)} %copy-done.12) | copy-start | bytes 6291460
  476.6 79.6 %reduce-scatter.30.cloned.1.call-start = ((), (), s32[]{:S(2)}) async-start(), calls=%async_computation.28 | async-start | bytes 4718592 | tf_op jit(solution)/shard_map/reduce_scatter | solution.py:258
  483.2 127.6 %reduce-scatter.32.cloned.1.call-start = ((), (), s32[]{:S(2)}) async-start(), calls=%async_computation.29 | async-start | bytes 4718592 | tf_op jit(solution)/shard_map/reduce_scatter | solution.py:258
  490.6 12.8 %copy-start.5 = (f32[128,1024]{1,0:T(8,128)S(1)}, f32[128,1024]{1,0:T(8,128)}, u32[]{:S(2)}) copy-start(f32[128,1024]{1,0:T(8,128)} %param.19) | copy-start | bytes 1572868
  490.6 12.8 %copy-start.65 = (f32[1,1024]{1,0:T(1,128)S(1)}, f32[1,1024]{1,0:T(1,128)}, u32[]{:S(2)}) copy-start(f32[1,1024]{1,0:T(1,128)} %copy-done.64) | copy-start | bytes 12292
  490.6 12.8 %copy-start.74 = (f32[128]{0:T(128)S(1)}, f32[128]{0:T(128)}, u32[]{:S(2)}) copy-start(f32[128]{0:T(128)} %copy-done.73) | copy-start | bytes 1540
  490.7 15.6 %copy-start.45 = (bf16[512,1024]{1,0:T(8,128)(2,1)S(1)}, bf16[512,1024]{1,0:T(8,128)(2,1)}, u32[]{:S(2)}) copy-start(bf16[512,1024]{1,0:T(8,128)(2,1)} %all-gather.8.cloned.1.call-done) | copy-start | bytes 3145732
  490.7 159.7 %reduce-scatter.24.cloned.1.call-start = ((), (), s32[]{:S(2)}) async-start(), calls=%async_computation.25 | async-start | bytes 1179648 | tf_op jit(solution)/shard_map/reduce_scatter | solution.py:315
  493.3 194.1 %reduce-scatter.34.cloned.1.call-start = ((), (), s32[]{:S(2)}) async-start(), calls=%async_computation.30 | async-start | bytes 589824
  506.2 226.1 %reduce-scatter.22.cloned.1.call-start = ((), (), s32[]{:S(2)}) async-start(), calls=%async_computation.24 | async-start | bytes 2359296 | tf_op jit(solution)/shard_map/reduce_scatter | solution.py:314
  508.3 298.6 %reduce-scatter.26.cloned.1.call-start = ((), (), s32[]{:S(2)}) async-start(), calls=%async_computation.26 | async-start | bytes 9437184 | tf_op jit(solution)/shard_map/reduce_scatter | solution.py:257
  517.1 364.5 %reduce-scatter.28.cloned.1.call-start = ((), (), s32[]{:S(2)}) async-start(), calls=%async_computation.27 | async-start | bytes 9437184 | tf_op jit(solution)/shard_map/reduce_scatter | solution.py:257
  534.9 76.9 %copy-start.19 = (f32[16,128,128]{2,1,0:T(8,128)S(1)}, f32[16,128,128]{2,1,0:T(8,128)}, u32[]{:S(2)}) copy-start(f32[16,128,128]{2,1,0:T(8,128)} %param.27) | copy-start | bytes 3145732
  616.0 40.0 %copy-start.40 = (f32[128,1024]{1,0:T(8,128)S(1)}, f32[128,1024]{1,0:T(8,128)}, u32[]{:S(2)}) copy-start(f32[128,1024]{1,0:T(8,128)} %get-tuple-element.178) | copy-start | bytes 1572868
  616.0 40.0 %copy-start.47 = (bf16[128,1024]{1,0:T(8,128)(2,1)S(1)}, bf16[128,1024]{1,0:T(8,128)(2,1)}, u32[]{:S(2)}) copy-start(bf16[128,1024]{1,0:T(8,128)(2,1)} %reduce-scatter.20.cloned.1.call-done) | copy-start | bytes 786436
  616.0 84.0 %copy-start.76 = (f32[2,128]{1,0:T(2,128)S(1)}, f32[2,128]{1,0:T(2,128)}, u32[]{:S(2)}) copy-start(f32[2,128]{1,0:T(2,128)} %param.23) | copy-start | bytes 3076
  616.0 84.0 %copy-start.77 = (f32[2,128]{1,0:T(2,128)S(1)}, f32[2,128]{1,0:T(2,128)}, u32[]{:S(2)}) copy-start(f32[2,128]{1,0:T(2,128)} %param.28) | copy-start | bytes 3076
  616.0 116.3 %copy-start.28 = (f32[4,128,128]{1,2,0:T(8,128)S(1)}, f32[4,128,128]{1,2,0:T(8,128)}, u32[]{:S(2)}) copy-start(f32[4,128,128]{1,2,0:T(8,128)} %copy-done.27) | copy-start | bytes 786436
  650.4 49.7 %copy-start.78 = (f32[2,128]{1,0:T(2,128)S(1)}, f32[2,128]{1,0:T(2,128)}, u32[]{:S(2)}) copy-start(f32[2,128]{1,0:T(2,128)} %param.29) | copy-start | bytes 3076
  700.0 108.2 %copy-start.75 = (f32[2,128]{1,0:T(2,128)}, f32[2,128]{1,0:T(2,128)S(1)}, u32[]{:S(2)}) copy-start(f32[2,128]{1,0:T(2,128)S(1)} %psum.7) | copy-start | bytes 3076
  (52 other events, 105.3 us)
Sparse Core Ops, SparseCore 0:
  21.9 28.2 all-gather.7
  52.7 22.8 all-gather.9
  86.0 43.6 reduce-scatter.13
  131.1 44.8 all-gather.17
  177.9 26.7 all-gather.11
  207.1 35.9 all-gather.13
  245.6 36.5 all-gather.15
  344.8 43.8 reduce-scatter.17
  409.2 27.5 reduce-scatter.15
  439.3 26.4 all-gather.19
  476.8 26.6 reduce-scatter.19
  506.7 49.5 reduce-scatter.29
  559.6 51.0 reduce-scatter.31
  614.4 35.9 reduce-scatter.23
  653.3 34.0 reduce-scatter.33
  691.2 41.0 reduce-scatter.21
  735.6 71.2 reduce-scatter.25
  810.2 71.2 reduce-scatter.27
